TPU v7x, 32 devices: a whole 2x2x4 slice. The times are simulated.
32 devices in a mesh: dom: 8 (over y, x, core), st: 4 (over z).
Axes of the slice: x: 2, y: 2, z: 4, core: 2. Of those that a mesh axis runs over, the one named last changes fastest.
Arguments:
- start_block: bfloat16 [2, 64, 128, 729], P(None, 'dom', 'st'), may hold values from -48 to 48
- resident: bfloat16 [1024, 64, 729], P('st', 'dom'), may hold values from -0.09375 to 0.09375
- stiffness: bfloat16 [729, 729], replicated, may hold values from -0.21875 to 0.21875
- cell_scale: float32 [64], P('dom'), may hold values from 0.5 to 2
- potential: float32 [64, 729], P('dom'), may hold values from -1 to 1
- cell_count: int32 [8], P('dom'), may hold values from 2 to 8, as said below
- face_index: int32 [8, 2, 81], P('dom'), may hold values from 0 to 5831, as said below
Outputs:
- rotated: bfloat16 [2, 64, 128, 729], P(None, 'dom', 'st')
Inputs may be any that keep to these rules, and one draw needn't show every extreme that they name: Domain d has cell_count[d] live cells in its first slots; some domain has 8 and some has 2. face_index[d, 0, :] lists each node of the last face of domain d's last live cell once, face_index[d, 1, :] each node of the first face of its cell 0 once, as flat indices cell * 729 + node; the k-th entries of face_index[d, 0] and face_index[d + 1, 1] are the same mesh node.
All inputs are finite; a program needn't handle non-finite values.
Results may differ from a plain program's by a relative error of at most 0.0075.
Values may be sent and summed in bfloat16 or wider, within the bound.
A program may use at most 64 MiB of HBM per device.

v0:
```python
from functools import partial

import jax
import jax.numpy as jnp
from jax import lax
from jax.sharding import PartitionSpec as P

CENTER = 0.5
HALF_WIDTH = 2.0
EPSILON = 1e-06


def with_halo(value, sides, width):
    for axis, dim in sides:
        devices, length = (lax.axis_size(axis), value.shape[dim])
        up = [(i, (i + 1) % devices) for i in range(devices - 1)]
        down = [(j, i) for i, j in up]
        last = lax.slice_in_dim(value, length - width, length, axis=dim)
        first = lax.slice_in_dim(value, 0, width, axis=dim)
        before = lax.ppermute(last, axis, up)
        after = lax.ppermute(first, axis, down)
        value = jnp.concatenate([before, value, after], axis=dim)
    return value


def apply_operator(in_field, stiffness, cell_scale, potential, live_cells, face_cells, face_nodes):
    slot_count, state_count, node_count = in_field.shape
    face_size = face_cells.shape[1]
    local_sum = jnp.dot(
        in_field.reshape(slot_count * state_count, node_count),
        stiffness,
        preferred_element_type=jnp.float32,
    ).reshape(slot_count, state_count, node_count)
    local_sum = cell_scale[:, None, None] * local_sum + potential[:, None, :] * in_field.astype(
        jnp.float32
    )
    right_face = local_sum[:-1, :, node_count - face_size :]
    left_face = local_sum[1:, :, :face_size]
    pair_live = live_cells[1:, None, None]
    local_sum = local_sum.at[:-1, :, node_count - face_size :].set(
        right_face + pair_live * left_face
    )
    local_sum = local_sum.at[1:, :, :face_size].set(left_face + pair_live * right_face)
    outgoing = jnp.stack(
        [local_sum[face_cells[1], :, face_nodes[1]], local_sum[face_cells[0], :, face_nodes[0]]]
    )
    padded = with_halo(outgoing, (("dom", 0),), 1)
    local_sum = local_sum.at[face_cells[1], :, face_nodes[1]].add(padded[0])
    local_sum = local_sum.at[face_cells[0], :, face_nodes[0]].add(padded[3])
    return local_sum * live_cells[:, None, None]


def mixing_exact(inner_product_matrix, total_nodes):
    mean_square = jnp.diagonal(inner_product_matrix) / total_nodes + EPSILON
    inverse_root = lax.rsqrt(mean_square)
    normed = inner_product_matrix * inverse_root[:, None] * inverse_root[None, :] / total_nodes
    identity = jnp.eye(inner_product_matrix.shape[0], dtype=jnp.float32)
    return inverse_root[:, None] * (1.5 * identity - 0.5 * normed)


def coefficients(correlation, inner_product_matrix, total_nodes):
    mixing = mixing_exact(inner_product_matrix, total_nodes)
    projected_states = jnp.dot(
        correlation, mixing, precision=lax.Precision.HIGHEST, preferred_element_type=jnp.float32
    )
    return (mixing.astype(jnp.bfloat16), projected_states.astype(jnp.bfloat16))


def filter_states(start_states, operator):
    start_wide = start_states.astype(jnp.float32)
    step_one = ((operator(start_states) - CENTER * start_wide) / HALF_WIDTH).astype(jnp.bfloat16)
    return (
        2.0 * (operator(step_one) - CENTER * step_one.astype(jnp.float32)) / HALF_WIDTH - start_wide
    ).astype(jnp.bfloat16)


def on_device(start_block, resident, stiffness, cell_scale, potential, cell_count, face_index):
    block_total, cell_cap, state_width, node_count = start_block.shape
    live_cells = (jnp.arange(cell_cap) < cell_count[0]).astype(jnp.float32)
    live_mask = live_cells.astype(jnp.bfloat16)[:, None, None]
    face_cells = face_index[0] // node_count
    face_nodes = face_index[0] % node_count
    total_nodes = float(lax.axis_size("dom") * cell_cap * node_count)
    operator = partial(
        apply_operator,
        stiffness=stiffness,
        cell_scale=cell_scale,
        potential=potential,
        live_cells=live_cells,
        face_cells=face_cells,
        face_nodes=face_nodes,
    )
    starts = start_block * live_mask[None]
    stacked = jnp.concatenate([starts[block_index] for block_index in range(block_total)], 1)
    filtered_all = filter_states(stacked, operator)
    filtered = [
        filtered_all[:, block_index * state_width : (block_index + 1) * state_width]
        for block_index in range(block_total)
    ]
    results = []
    first_state = lax.axis_index("st") * state_width
    for block_states in filtered:
        every_state_rows = lax.all_gather(block_states, "st", axis=1, tiled=True)
        correlation = jnp.einsum(
            "jpu,pzu->jz", resident, every_state_rows, preferred_element_type=jnp.float32
        )
        inner_product_matrix = jnp.einsum(
            "ptw,phw->th", every_state_rows, every_state_rows, preferred_element_type=jnp.float32
        )
        correlation, inner_product_matrix = lax.psum((correlation, inner_product_matrix), "dom")
        mixing, projected_states = coefficients(correlation, inner_product_matrix, total_nodes)
        series_term_sum = jnp.einsum(
            "es,evd->vsd", projected_states, resident, preferred_element_type=jnp.float32
        )
        own_terms = lax.psum_scatter(
            series_term_sum.astype(jnp.bfloat16), "st", scatter_dimension=1, tiled=True
        ).astype(jnp.float32)
        self_mixing_weight = lax.dynamic_slice_in_dim(mixing, first_state, state_width, 1)
        retained_portion = jnp.einsum(
            "ghy,hw->gwy", every_state_rows, self_mixing_weight, preferred_element_type=jnp.float32
        )
        results.append((retained_portion - own_terms).astype(jnp.bfloat16) * live_mask)
    return jnp.stack(results)


def solution(mesh):
    return jax.shard_map(
        on_device,
        mesh=mesh,
        in_specs=(
            P(None, "dom", "st", None),
            P("st", "dom", None),
            P(),
            P("dom"),
            P("dom", None),
            P("dom"),
            P("dom", None, None),
        ),
        out_specs=P(None, "dom", "st", None),
        check_vma=False,
    )
```

profile of v0, /device:TPU:0, one launch (start us, length us, event | category | flops | bytes accessed | tf_op | source)
XLA Modules:
  0.0 346.1 jit_solution(2968645453988374840)
XLA Ops:
  13.6 2.8 multiply_add_fusion.1
  16.4 3.6 %scatter.14 = f32[8,64,729]{2,1,0:T(8,128)} dynamic-update-slice(f32[8,64,729]{2,1,0:T(8,128)} %copy-done.5, f32[7,64,81]{2,1,0:T(8,128)} %get-tuple-element.60, s32[]{:T(128)} %bitcast.4, s32[]{:T(128)} %constant.145.clone.1, s32[]{:T(128)} %bitcast.5) | dynamic-update-slice | bytes 290308 | tf_op jit(solution)/shard_map/scatter | solution.py:40
  22.1 3.2 copy.56
  25.4 3.4 gather_fusion
  28.7 3.0 collective-permute-start
  31.8 3.4 gather_fusion.1
  36.4 10.5 %scatter_fusion = f32[8,64,729]{1,0,2:T(8,128)} fusion(f32[8,64,729]{1,0,2:T(8,128)} %copy.56, s32[81]{0:T(128)S(1)} %get-tuple-element.68, f32[81,64]{1,0:T(8,128)} %bitcast.16), kind=kCustom, calls=%fused_computation.6 | custom fusion | flops 5184 | bytes 62856 | tf_op jit(solution)/shard_map/scatter-add | solution.py:48
  47.0 10.4 %scatter_fusion.1 = f32[8,64,729]{1,0,2:T(8,128)} fusion(f32[8,64,729]{1,0,2:T(8,128)} %scatter_fusion, s32[81]{0:T(128)S(1)} %get-tuple-element.67, f32[81,64]{1,0:T(8,128)S(1)} %bitcast.139), kind=kCustom, calls=%fused_computation.7 | custom fusion | flops 5184 | bytes 62856 | tf_op jit(solution)/shard_map/scatter-add | solution.py:49
  57.4 3.3 copy.58
  60.7 3.5 %fusion.4 = f32[8,64,729]{2,1,0:T(8,128)S(1)} fusion(bf16[729,729]{1,0:T(8,128)(2,1)} %param.17, f32[8,729]{1,0:T(8,128)S(1)} %copy-done.12, f32[8]{0:T(128)S(1)} %copy-done.13, bf16[8,32,729]{2,1,0:T(8,128)(2,1)} %copy-done.6, bf16[8,32,729]{2,1,0:T(8,128)(2,1)S(1)} %get-tuple-element.63, f32[8,64,729]{2,1,0:T(8,128)} %copy.58, f32[8]{0:T(128)S(1)} %get-tuple-element.73), kind=kOutput, calls=%fused_computation.21 | convolution fusion | flops 552407040 | bytes 4818754 | tf_op jit(solution)/shard_map/dot_general | solution.py:29
  65.3 2.8 multiply_add_fusion
  68.2 3.7 %scatter.16 = f32[8,64,729]{2,1,0:T(8,128)} dynamic-update-slice(f32[8,64,729]{2,1,0:T(8,128)} %copy-done.4, f32[7,64,81]{2,1,0:T(8,128)} %get-tuple-element.58, s32[]{:T(128)} %bitcast.4, s32[]{:T(128)} %constant.145.clone.1, s32[]{:T(128)} %bitcast.5) | dynamic-update-slice | bytes 290308 | tf_op jit(solution)/shard_map/scatter | solution.py:40
  71.9 2.1 scatter.19
  73.9 3.2 copy.60
  77.1 3.4 gather_fusion.2
  80.5 5.1 %collective-permute-start.2 = (f32[1,81,64]{2,1,0:T(8,128)S(1)}, f32[1,81,64]{2,1,0:T(8,128)}, u32[]{:S(2)}, u32[]{:S(2)}) collective-permute-start(f32[1,81,64]{2,1,0:T(8,128)S(1)} %bitcast.136), channel_id=1, source_target_pairs={{0,4},{4,8},{8,12},{12,16},{16,20},{20,24},{24,28},{1,5},{5,9},{9,... | collective-permute-start | bytes 62216 | tf_op jit(solution)/shard_map/ppermute | solution.py:20
  85.6 3.4 gather_fusion.3
  90.5 10.6 %scatter_fusion.2 = f32[8,64,729]{1,0,2:T(8,128)} fusion(f32[8,64,729]{1,0,2:T(8,128)} %copy.60, s32[81]{0:T(128)S(1)} %get-tuple-element.68, f32[81,64]{1,0:T(8,128)} %bitcast.22), kind=kCustom, calls=%fused_computation.8 | custom fusion | flops 5184 | bytes 62856 | tf_op jit(solution)/shard_map/scatter-add | solution.py:48
  101.1 10.4 %scatter_fusion.3 = f32[8,64,729]{1,0,2:T(8,128)} fusion(f32[8,64,729]{1,0,2:T(8,128)} %scatter_fusion.2, s32[81]{0:T(128)S(1)} %get-tuple-element.67, f32[81,64]{1,0:T(8,128)S(1)} %bitcast.138), kind=kCustom, calls=%fused_computation.9 | custom fusion | flops 5184 | bytes 62856 | tf_op jit(solution)/shard_map/scatter-add | solution.py:49
  111.5 3.3 copy.62
  114.8 2.6 fusion.10
  119.2 40.4 %all-gather.5.cloned.1.call-done = bf16[8,128,729]{2,1,0:T(8,128)(2,1)} async-done(((bf16[8,32,729]{2,1,0:T(8,128)(2,1)}), bf16[8,128,729]{2,1,0:T(8,128)(2,1)}) %all-gather.5.cloned.1.call-update) | async-done | bytes 1493008 | tf_op jit(solution)/shard_map/all_gather | solution.py:103
  159.5 3.3 convolution_bitcast_fusion.2
  164.7 32.3 %all-gather.3.cloned.1.call-done = bf16[8,128,729]{2,1,0:T(8,128)(2,1)} async-done(((bf16[8,32,729]{2,1,0:T(8,128)(2,1)}), bf16[8,128,729]{2,1,0:T(8,128)(2,1)}) %all-gather.3.cloned.1.call-update) | async-done | bytes 1493008 | tf_op jit(solution)/shard_map/all_gather | solution.py:103
  197.0 3.4 fusion.21
  201.7 53.8 %all-reduce.3.cloned.1.call-done = (f32[256,128]{0,1:T(8,128)}, f32[128,128]{1,0:T(8,128)}, f32[256,128]{0,1:T(8,128)}, f32[128,128]{1,0:T(8,128)}) async-done(((f32[256,128]{0,1:T(8,128)}, f32[128,128]{1,0:T(8,128)}, f32[256,128]{0,1:T(8,128)}, f32[128,128]{1,0:T(8,128)}), (f32[256,128]{0,1:T(8,128)}, f32[128,128]{1,0:T(8,128)}, f32[256,128]{0,1:T(8,128)}, ...) | async-done | bytes 393232 | tf_op jit(solution)/shard_map/psum | solution.py:110
  259.7 2.1 fusion.11
  261.8 3.4 copy.67
  267.0 2.1 fusion.12
  269.1 3.4 copy.73
  272.5 27.6 %reduce-scatter.3.cloned.1.call-done = bf16[8,32,729]{2,0,1:T(8,128)(2,1)} async-done(((bf16[8,128,729]{2,0,1:T(8,128)(2,1)}), bf16[8,32,729]{2,0,1:T(8,128)(2,1)}) %reduce-scatter.3.cloned.1.call-update) | async-done | bytes 373264 | tf_op jit(solution)/shard_map/reduce_scatter | solution.py:115
  302.1 34.6 %reduce-scatter.5.cloned.1.call-done = bf16[8,32,729]{2,0,1:T(8,128)(2,1)} async-done(((bf16[8,128,729]{2,0,1:T(8,128)(2,1)}), bf16[8,32,729]{2,0,1:T(8,128)(2,1)}) %reduce-scatter.5.cloned.1.call-update) | async-done | bytes 373264 | tf_op jit(solution)/shard_map/reduce_scatter | solution.py:115
  (70 shorter events, 27.8 us)
Async XLA Ops:
  6.5 156.3 %copy-start = (bf16[256,8,729]{0,1,2:T(8,128)(2,1)S(1)}, bf16[256,8,729]{0,1,2:T(8,128)(2,1)}, u32[]{:S(2)}) copy-start(bf16[256,8,729]{0,1,2:T(8,128)(2,1)} %param.16) | copy-start | bytes 8957956
  6.5 153.0 %all-gather.5.cloned.1.call-start = ((), (), s32[]{:S(2)}) async-start(), calls=%async_computation.4 | async-start | bytes 1966080 | tf_op jit(solution)/shard_map/all_gather | solution.py:103
  7.4 2.2 copy-start.9
  7.4 4.2 %copy-start.10 = (bf16[729,729]{1,0:T(8,128)(2,1)S(1)}, bf16[729,729]{1,0:T(8,128)(2,1)}, u32[]{:S(2)}) copy-start(bf16[729,729]{1,0:T(8,128)(2,1)} %param.17) | copy-start | bytes 3188650
  7.4 4.2 %copy-start.11 = (f32[8,729]{1,0:T(8,128)S(1)}, f32[8,729]{1,0:T(8,128)}, u32[]{:S(2)}) copy-start(f32[8,729]{1,0:T(8,128)} %param.19) | copy-start | bytes 69988
  7.4 4.2 %copy-start.13 = (f32[8]{0:T(128)S(1)}, f32[8]{0:T(128)}, u32[]{:S(2)}) copy-start(f32[8]{0:T(128)} %param.18) | copy-start | bytes 100
  8.8 3.6 %copy-start.6 = (bf16[8,32,729]{2,1,0:T(8,128)(2,1)}, bf16[8,32,729]{2,1,0:T(8,128)(2,1)S(1)}, u32[]{:S(2)}) copy-start(bf16[8,32,729]{2,1,0:T(8,128)(2,1)S(1)} %get-tuple-element.64) | copy-start | bytes 1119748
  12.4 1.2 copy-start.5
  22.1 3.2 copy-start.8
  28.7 7.7 %collective-permute-start = (f32[1,81,64]{2,1,0:T(8,128)S(1)}, f32[1,81,64]{2,1,0:T(8,128)}, u32[]{:S(2)}, u32[]{:S(2)}) collective-permute-start(f32[1,81,64]{2,1,0:T(8,128)S(1)} %bitcast.137), channel_id=1, source_target_pairs={{0,4},{4,8},{8,12},{12,16},{16,20},{20,24},{24,28},{1,5},{5,9},{9,... | collective-permute-start | bytes 62216 | tf_op jit(solution)/shard_map/ppermute | solution.py:20
  35.1 11.8 %collective-permute-start.1 = (f32[1,81,64]{2,1,0:T(8,128)S(1)}, f32[1,81,64]{2,1,0:T(8,128)S(1)}, u32[]{:S(2)}, u32[]{:S(2)}) collective-permute-start(f32[1,81,64]{2,1,0:T(8,128)S(1)} %bitcast.135), channel_id=1, source_target_pairs={{4,0},{8,4},{12,8},{16,12},{20,16},{24,20},{28,24},{5,1},{9,5},{13... | collective-permute-start | bytes 62216 | tf_op jit(solution)/shard_map/ppermute | solution.py:21
  57.4 3.3 copy-start.12
  64.2 1.2 copy-start.4
  80.5 10.0 %collective-permute-start.2 = (f32[1,81,64]{2,1,0:T(8,128)S(1)}, f32[1,81,64]{2,1,0:T(8,128)}, u32[]{:S(2)}, u32[]{:S(2)}) collective-permute-start(f32[1,81,64]{2,1,0:T(8,128)S(1)} %bitcast.136), channel_id=1, source_target_pairs={{0,4},{4,8},{8,12},{12,16},{16,20},{20,24},{24,28},{1,5},{5,9},{9,... | collective-permute-start | bytes 62216 | tf_op jit(solution)/shard_map/ppermute | solution.py:20
  89.0 12.1 %collective-permute-start.3 = (f32[1,81,64]{2,1,0:T(8,128)S(1)}, f32[1,81,64]{2,1,0:T(8,128)S(1)}, u32[]{:S(2)}, u32[]{:S(2)}) collective-permute-start(f32[1,81,64]{2,1,0:T(8,128)S(1)} %bitcast.134), channel_id=1, source_target_pairs={{4,0},{8,4},{12,8},{16,12},{20,16},{24,20},{28,24},{5,1},{9,5},{13... | collective-permute-start | bytes 62216 | tf_op jit(solution)/shard_map/ppermute | solution.py:21
  118.4 78.7 %all-gather.3.cloned.1.call-start = ((), (), s32[]{:S(2)}) async-start(), calls=%async_computation.2 | async-start | bytes 1966080 | tf_op jit(solution)/shard_map/all_gather | solution.py:103
  119.1 136.4 %all-reduce.3.cloned.1.call-start = ((), (), s32[]{:S(2)}) async-start(), calls=%async_computation.6 | async-start | bytes 786432 | tf_op jit(solution)/shard_map/psum | solution.py:110
  159.5 3.3 copy-start.1
  197.0 3.4 copy-start.2
  201.6 98.5 %reduce-scatter.3.cloned.1.call-start = ((), (), s32[]{:S(2)}) async-start(), calls=%async_computation.3 | async-start | bytes 1966080 | tf_op jit(solution)/shard_map/reduce_scatter | solution.py:115
  261.8 3.5 %copy-start.3 = (f32[128,128]{1,0:T(8,128)S(1)}, f32[128,128]{1,0:T(8,128)}, u32[]{:S(2)}) copy-start(f32[128,128]{1,0:T(8,128)} %get-tuple-element.54) | copy-start | bytes 196612
  265.2 1.4 copy-start.7
  265.2 71.4 %reduce-scatter.5.cloned.1.call-start = ((), (), s32[]{:S(2)}) async-start(), calls=%async_computation.5 | async-start | bytes 1966080 | tf_op jit(solution)/shard_map/reduce_scatter | solution.py:115
Sparse Core Ops, SparseCore 0:
  118.5 41.0 all-gather.4
  161.1 35.8 all-gather.2
  201.7 53.7 all-reduce.2
  265.3 34.7 reduce-scatter.2
  302.3 34.2 reduce-scatter.4
where the time goes:
time: 348 us; the launch traced here: 346 us
  waiting for transfers between devices  190 us (55%)
  other arithmetic  55.7 us (16%)
  local copies, waits for them, and re-layouts  52 us (15%)
  matrix products  23.6 us (7%)
  between operations  14.2 us (4%)
  starting transfers between devices  11 us (3%)
    all_gather x2, waiting for transfers between devices, on_device(): every_state_rows = lax.all_gather(block_states, 'st', axis=1, tiled=True)  72.7 us
    reduce_scatter x2, waiting for transfers between devices, on_device(): lax.psum_scatter(series_term_sum.astype(jnp.bfloat16), 'st', scatter_dime...  62.2 us
    psum x1, waiting for transfers between devices, on_device(): lax.psum((correlation, inner_product_matrix), 'dom')  53.8 us
    scatter-add x2, other arithmetic, apply_operator(): local_sum = local_sum.at[face_cells[1], :, face_nodes[1]].add(padded[0])  21.1 us
    scatter-add x2, other arithmetic, apply_operator(): local_sum = local_sum.at[face_cells[0], :, face_nodes[0]].add(padded[3])  20.9 us
    scatter x4, local copies, waits for them, and re-layouts, apply_operator(): local_sum.at[1:, :, :face_size].set(left_face + pair_live * right_face)  10.5 us
    ppermute x2, starting transfers between devices, with_halo(): before = lax.ppermute(last, axis, up)  8.11 us
    scatter x2, local copies, waits for them, and re-layouts, apply_operator(): local_sum.at[:-1, :, node_count - face_size:]  7.35 us
  transfers between devices with their start and end apart: 9, of which 5 were waited for; matrix products, arithmetic and copies ran while one was open for 12% of the time, Pallas kernels for 0%

commit v1 on v0

v1 whole, which is shorter than its diff:
```python
from functools import partial

import jax
import jax.numpy as jnp
from jax import lax
from jax.experimental import pallas as pl
from jax.experimental.pallas import tpu as pltpu
from jax.sharding import PartitionSpec as P

CENTER = 0.5
HALF_WIDTH = 2.0
EPSILON = 1e-06
F32 = jnp.float32
BF16 = jnp.bfloat16
RIGHT, LEFT = 0, 1


def dot_nn(a, b, precision=None):
    return lax.dot_general(
        a, b, (((1,), (0,)), ((), ())), precision=precision, preferred_element_type=F32
    )


def dot_nt(a, b, precision=None):
    return lax.dot_general(
        a, b, (((1,), (1,)), ((), ())), precision=precision, preferred_element_type=F32
    )


def kernel(
    sizes,
    flags_ref,
    start_ref,
    res_ref,
    stiff_ref,
    pot_ref,
    face_ref,
    out_ref,
    local,
    inner,
    states,
    part,
    part_recv,
    total,
    mix,
    proj,
    share,
    share_recv,
    face_out,
    face_in,
    face_send_sem,
    face_recv_sem,
    gather_send_sem,
    gather_recv_sem,
    one_send_sem,
    one_recv_sem,
    two_send_sem,
    two_recv_sem,
    share_send_sem,
    share_recv_sem,
):
    doms, sts, blocks, cells, width, nodes, face, res, rows = sizes
    total_states = sts * width
    total_nodes = float(doms * cells * nodes)
    window = (nodes - face) // 128 * 128
    offset = nodes - face - window
    d = lax.axis_index("dom")
    s = lax.axis_index("st")
    has_right, has_left = s < sts - 1, s > 0
    has_next, has_prev = d < doms - 1, d > 0
    own = pl.ds(pl.multiple_of(s * width, width), width)
    pending = []

    def dom_peer(k):
        return lax.rem(d + k, doms)

    barrier = pltpu.get_barrier_semaphore()

    def greet(k, carry):
        pl.semaphore_signal(
            barrier, inc=1, device_id={"dom": dom_peer(k)}, device_id_type=pl.DeviceIdType.MESH
        )
        return carry

    lax.fori_loop(1, doms, greet, 0)

    @pl.when(has_right)
    def _():
        pl.semaphore_signal(
            barrier, inc=1, device_id={"st": s + 1}, device_id_type=pl.DeviceIdType.MESH
        )

    @pl.when(has_left)
    def _():
        pl.semaphore_signal(
            barrier, inc=1, device_id={"st": s - 1}, device_id_type=pl.DeviceIdType.MESH
        )

    neighbours = has_right.astype(jnp.int32) + has_left.astype(jnp.int32)
    pl.semaphore_wait(barrier, doms - 1 + neighbours)

    def remote(src, dst, send_sem, recv_sem, axis, peer):
        return pltpu.make_async_remote_copy(
            src_ref=src,
            dst_ref=dst,
            send_sem=send_sem,
            recv_sem=recv_sem,
            device_id={axis: peer},
            device_id_type=pl.DeviceIdType.MESH,
        )

    def one_hot(row, first, count):
        node = lax.broadcasted_iota(jnp.int32, (count, face), 0) + first
        return jnp.where(face_ref[row : row + 1, :] == node, 1.0, 0.0).astype(F32)

    def rows_of(c):
        return slice(c * width, (c + 1) * width)

    def face_copy(step, b, way):
        return remote(
            face_out.at[step, b, way],
            face_in.at[step, b, way],
            face_send_sem.at[step, b, way],
            face_recv_sem.at[step, b, way],
            "dom",
            d + 1 if way == RIGHT else d - 1,
        )

    def apply_operator(step, b, field):
        local[...] = dot_nn(field(None), stiff_ref[...])
        last_tail = jnp.zeros((width, nodes - window), F32)
        for c in range(cells):
            value = flags_ref[0, c] * local[rows_of(c), :] + pot_ref[c : c + 1, :] * field(
                c
            ).astype(F32)
            local[rows_of(c), :] = value
            last_tail = last_tail + flags_ref[3, c] * value[:, window:]
        face_out[step, b, RIGHT] = dot_nn(
            last_tail, one_hot(0, window, nodes - window), lax.Precision.HIGHEST
        )
        face_out[step, b, LEFT] = dot_nn(
            local[rows_of(0), :face], one_hot(1, 0, face), lax.Precision.HIGHEST
        )
        for way, there in ((RIGHT, has_next), (LEFT, has_prev)):

            @pl.when(there)
            def _():
                face_copy(step, b, way).start()

            pending.append((there, partial(face_copy, step, b, way)))
        for c in range(cells - 1):
            pair = flags_ref[2, c + 1]
            tail = local[rows_of(c), window:]
            head = local[rows_of(c + 1), :face]
            padded = head
            if offset:
                padded = jnp.concatenate([jnp.zeros((width, offset), F32), head], axis=1)
            local[rows_of(c), window:] = tail + pair * padded
            local[rows_of(c + 1), :face] = head + pair * tail[:, offset:]
        for way, source in ((RIGHT, has_prev), (LEFT, has_next)):

            @pl.when(source)
            def _():
                face_copy(step, b, way).wait_recv()

            @pl.when(jnp.logical_not(source))
            def _():
                face_in[step, b, way] = jnp.zeros((width, face), F32)

        local[rows_of(0), :face] += dot_nt(
            face_in[step, b, RIGHT], one_hot(1, 0, face), lax.Precision.HIGHEST
        )
        tail_add = dot_nt(
            face_in[step, b, LEFT], one_hot(0, window, nodes - window), lax.Precision.HIGHEST
        )
        for c in range(cells):
            local[rows_of(c), window:] += flags_ref[3, c] * tail_add

    def filter_block(b):
        def first(c):
            if c is None:
                parts = [first(i) for i in range(cells)]
                return jnp.concatenate(parts, axis=0)
            return start_ref[b, c] * flags_ref[1, c].astype(BF16)

        def second(c):
            return inner[...] if c is None else inner[rows_of(c), :]

        apply_operator(0, b, first)
        for c in range(cells):
            value = flags_ref[1, c] * local[rows_of(c), :]
            inner[rows_of(c), :] = ((value - CENTER * first(c).astype(F32)) / HALF_WIDTH).astype(
                BF16
            )
        apply_operator(1, b, second)
        for c in range(cells):
            value = flags_ref[1, c] * local[rows_of(c), :]
            states[b, c, own, :] = (
                2.0 * (value - CENTER * second(c).astype(F32)) / HALF_WIDTH - first(c).astype(F32)
            ).astype(BF16)

    def gather_copy(b, way, shard):
        at = states.at[b, :, pl.ds(pl.multiple_of(shard * width, width), width), :]
        return remote(
            at,
            at,
            gather_send_sem.at[b, way, shard],
            gather_recv_sem.at[b, shard],
            "st",
            s + 1 if way == RIGHT else s - 1,
        )

    def gather_send(b, way, shard, there):
        @pl.when(there)
        def _():
            gather_copy(b, way, shard).start()

        pending.append((there, partial(gather_copy, b, way, shard)))

    def gather_start(b):
        gather_send(b, RIGHT, s, has_right)
        gather_send(b, LEFT, s, has_left)

    def gather_steps(b):
        for k in range(1, sts):
            for way, shard, here, more in (
                (RIGHT, s - k, s >= k, has_right),
                (LEFT, s + k, s + k < sts, has_left),
            ):

                @pl.when(here)
                def _():
                    gather_copy(b, way, shard).wait_recv()

                gather_send(b, way, shard, jnp.logical_and(here, more))

    def contract(b):
        part[b] = jnp.zeros(part.shape[1:], F32)

        def add_cell(c, carry):
            block = states[b, c]
            part[b, :res, :] += dot_nt(res_ref[c], block)
            part[b, res : res + total_states, :] += dot_nt(block, block)
            return carry

        lax.fori_loop(0, cells, add_cell, 0)

    def slice_of(peer):
        return pl.ds(pl.multiple_of(peer * rows, 8), rows)

    def one_copy(b, k):
        peer = dom_peer(k)
        return remote(
            part.at[b, slice_of(peer)],
            part_recv.at[b, k],
            one_send_sem.at[b, k],
            one_recv_sem.at[b, k],
            "dom",
            peer,
        )

    def two_copy(b, k):
        at = total.at[b, slice_of(d)]
        return remote(
            at, at, two_send_sem.at[b, k], two_recv_sem.at[b, k], "dom", dom_peer(k)
        )

    def from_peer(b, k):
        at = total.at[b, slice_of(dom_peer(doms - k))]
        return remote(
            at, at, two_send_sem.at[b, k], two_recv_sem.at[b, k], "dom", dom_peer(doms - k)
        )

    def all_reduce(b):
        def loop(body):
            def step(k, carry):
                body(k)
                return carry

            lax.fori_loop(1, doms, step, 0)

        loop(lambda k: one_copy(b, k).start())
        total[b, slice_of(d), :] = part[b, slice_of(d), :]

        def add(k):
            one_copy(b, k).wait_recv()
            total[b, slice_of(d), :] += part_recv[b, k]

        loop(add)
        loop(lambda k: two_copy(b, k).start())
        loop(lambda k: from_peer(b, k).wait_recv())

    def finish_reduce(b):
        def step(k, carry):
            one_copy(b, k).wait_send()
            two_copy(b, k).wait_send()
            return carry

        lax.fori_loop(1, doms, step, 0)

    def coefficients(b):
        gram = total[b, res : res + total_states, :]
        shape = (total_states, total_states)
        eye = (
            lax.broadcasted_iota(jnp.int32, shape, 0) == lax.broadcasted_iota(jnp.int32, shape, 1)
        ).astype(F32)
        along = jnp.sum(gram * eye, axis=0, keepdims=True) / total_nodes + EPSILON
        down = jnp.sum(gram * eye, axis=1, keepdims=True) / total_nodes + EPSILON
        root_i, root_j = lax.rsqrt(along), lax.rsqrt(down)
        mixing = root_i * (1.5 * eye - 0.5 * (gram * root_i * root_j / total_nodes))
        mix[b] = mixing.astype(BF16)
        proj[b] = dot_nt(mixing, total[b, :res, :], lax.Precision.HIGHEST).astype(BF16)

    def share_copy(b, t, way):
        return remote(
            share.at[b, t],
            share_recv.at[way, b, t],
            share_send_sem.at[b, t],
            share_recv_sem.at[way, b, t],
            "st",
            s + 1 if way == RIGHT else s - 1,
        )

    def targets():
        for j in range(sts - 1):
            far = sts - 1 - j
            yield far, RIGHT, far > s, has_left
            yield j, LEFT, j < s, has_right

    def share_start(b):
        for t, way, ahead, behind in targets():

            @pl.when(ahead)
            def _():
                def one(c, carry):
                    share[b, t, c] = dot_nn(
                        proj[b, t * width : (t + 1) * width, :], res_ref[c]
                    ).astype(BF16)
                    return carry

                lax.fori_loop(0, cells, one, 0)

            @pl.when(jnp.logical_and(ahead, jnp.logical_not(behind)))
            def _():
                share_copy(b, t, way).start()

            pending.append((ahead, partial(share_copy, b, t, way)))

    def share_forward(b):
        for t, way, ahead, behind in targets():

            @pl.when(jnp.logical_and(ahead, behind))
            def _():
                share_copy(b, t, way).wait_recv()

                def one(c, carry):
                    share[b, t, c] = (
                        share[b, t, c].astype(F32) + share_recv[way, b, t, c].astype(F32)
                    ).astype(BF16)
                    return carry

                lax.fori_loop(0, cells, one, 0)
                share_copy(b, t, way).start()

    def finish(b):
        def own_copy(way):
            return remote(
                share.at[b, s],
                share_recv.at[way, b, s],
                share_send_sem.at[b, s],
                share_recv_sem.at[way, b, s],
                "st",
                s + 1 if way == RIGHT else s - 1,
            )

        for c in range(cells):
            local[rows_of(c), :] = dot_nn(mix[b, own, :], states[b, c]) - dot_nn(
                proj[b, own, :], res_ref[c]
            )
        for way, source in ((RIGHT, has_left), (LEFT, has_right)):

            @pl.when(source)
            def _():
                own_copy(way).wait_recv()
                for c in range(cells):
                    local[rows_of(c), :] -= share_recv[way, b, s, c].astype(F32)

        for c in range(cells):
            out_ref[b, c] = local[rows_of(c), :].astype(BF16) * flags_ref[1, c].astype(BF16)

    filter_block(0)
    gather_start(0)
    for b in range(1, blocks):
        filter_block(b)
    for b in range(blocks):
        gather_steps(b)
        if b + 1 < blocks:
            gather_start(b + 1)
        contract(b)
        all_reduce(b)
        if b:
            share_forward(b - 1)
        coefficients(b)
        share_start(b)
        if b:
            finish(b - 1)
    share_forward(blocks - 1)
    finish(blocks - 1)
    for there, make in pending:

        @pl.when(there)
        def _():
            make().wait_send()

    for b in range(blocks):
        finish_reduce(b)


def on_device(start_block, resident, stiffness, cell_scale, potential, cell_count, face_index):
    blocks, cells, width, nodes = start_block.shape
    res = resident.shape[0]
    face = face_index.shape[2]
    doms, sts = lax.axis_size("dom"), lax.axis_size("st")
    total_states = sts * width
    rows = -(-(res + total_states) // (8 * doms)) * 8
    slot = jnp.arange(cells)
    live = (slot < cell_count[0]).astype(F32)
    last = (slot == cell_count[0] - 1).astype(F32)
    flags = jnp.stack([cell_scale, live, live, last])
    face_nodes = face_index[0] % nodes
    sizes = (doms, sts, blocks, cells, width, nodes, face, res, rows)
    dma = pltpu.SemaphoreType.DMA
    vmem = pl.BlockSpec(memory_space=pltpu.VMEM)
    return pl.pallas_call(
        partial(kernel, sizes),
        out_shape=jax.ShapeDtypeStruct((blocks, cells, width, nodes), BF16),
        in_specs=[pl.BlockSpec(memory_space=pltpu.SMEM)] + [vmem] * 5,
        out_specs=vmem,
        scratch_shapes=[
            pltpu.VMEM((cells * width, nodes), F32),
            pltpu.VMEM((cells * width, nodes), BF16),
            pltpu.VMEM((blocks, cells, total_states, nodes), BF16),
            pltpu.VMEM((blocks, doms * rows, total_states), F32),
            pltpu.VMEM((blocks, doms, rows, total_states), F32),
            pltpu.VMEM((blocks, doms * rows, total_states), F32),
            pltpu.VMEM((blocks, total_states, total_states), BF16),
            pltpu.VMEM((blocks, total_states, res), BF16),
            pltpu.VMEM((blocks, sts, cells, width, nodes), BF16),
            pltpu.VMEM((2, blocks, sts, cells, width, nodes), BF16),
            pltpu.VMEM((2, blocks, 2, width, face), F32),
            pltpu.VMEM((2, blocks, 2, width, face), F32),
            dma((2, blocks, 2)),
            dma((2, blocks, 2)),
            dma((blocks, 2, sts)),
            dma((blocks, sts)),
            dma((blocks, doms)),
            dma((blocks, doms)),
            dma((blocks, doms)),
            dma((blocks, doms)),
            dma((blocks, sts)),
            dma((2, blocks, sts)),
        ],
        compiler_params=pltpu.CompilerParams(
            collective_id=0, has_side_effects=True, vmem_limit_bytes=60 * 1024 * 1024
        ),
    )(
        flags,
        start_block,
        jnp.transpose(resident, (1, 0, 2)),
        stiffness,
        potential,
        face_nodes,
    )


def solution(mesh):
    return jax.shard_map(
        on_device,
        mesh=mesh,
        in_specs=(
            P(None, "dom", "st", None),
            P("st", "dom", None),
            P(),
            P("dom"),
            P("dom", None),
            P("dom"),
            P("dom", None, None),
        ),
        out_specs=P(None, "dom", "st", None),
        check_vma=False,
    )
```

time: 348 us -> 142 us (0.41)
  waiting for transfers between devices: 190 us -> 0 us
  Pallas kernels: 0 us -> 131 us
  other arithmetic: 55.7 us -> 2.48 us
  local copies, waits for them, and re-layouts: 52 us -> 7.06 us
  matrix products: 23.6 us -> 0 us
  between operations: 14.2 us -> 0.67 us
  starting transfers between devices: 11 us -> 0 us
    pallas_call x0 -> x1, Pallas kernels: none -> 131 us  [on_device(): pl.pallas_call(partial(kernel, sizes), out_shape=jax.ShapeDtypeStruct((bl...]
    all_gather x2 -> x0, waiting for transfers between devices: 72.7 us -> none  [on_device(): every_state_rows = lax.all_gather(block_states, 'st', axis=1, tiled=True)]
    reduce_scatter x2 -> x0, waiting for transfers between devices: 62.2 us -> none  [on_device(): lax.psum_scatter(series_term_sum.astype(jnp.bfloat16), 'st', scatter_dime...]
    psum x1 -> x0, waiting for transfers between devices: 53.8 us -> none  [on_device(): lax.psum((correlation, inner_product_matrix), 'dom')]
    scatter-add x4 -> x0, other arithmetic: 42 us -> none  [the longest x2 21.1 us: apply_operator(): local_sum = local_sum.at[face_cells[1], :, face_nodes[1]].add(padded[0])]
    dot_general x12 -> x0, matrix products: 23.6 us -> none  [the longest x2 5.19 us: on_device(): jnp.einsum('jpu,pzu->jz', resident, every_state_rows, preferred_element_t...]
    scatter x6 -> x0, local copies, waits for them, and re-layouts: 17.9 us -> none  [the longest x4 10.5 us: apply_operator(): local_sum.at[1:, :, :face_size].set(left_face + pair_live * right_face)]
    gather x6 -> x0, local copies, waits for them, and re-layouts: 16.7 us -> none  [the longest x2 6.74 us: apply_operator(): local_sum[face_cells[0], :, face_nodes[0]]]
  transfers between devices with their start and end apart: 9 -> 0, of which waited for: 5 -> 0; matrix products, arithmetic and copies ran while one was open for 12% -> 0% of each run, Pallas kernels for 0% -> 0%
where the time goes in v1:
time: 142 us
  Pallas kernels  131 us (92%)
  local copies, waits for them, and re-layouts  7.06 us (5%)
  other arithmetic  2.48 us (2%)
    pallas_call x1, Pallas kernels, on_device(): pl.pallas_call(partial(kernel, sizes), out_shape=jax.ShapeDtypeStruct((bl...  131 us
    unnamed x2, local copies, waits for them, and re-layouts  7.06 us

profile of v1, /device:TPU:0, one launch (start us, length us, event | category | flops | bytes accessed | tf_op | source)
XLA Modules:
  0.0 141.6 jit_solution(9282679837581618505)
XLA Ops:
  0.7 1.2 pad_maximum_fusion.flags_ref
  1.9 1.2 and_select_fusion.face_ref
  3.1 5.0 %copy.8 = bf16[256,8,729]{2,0,1:T(8,128)(2,1)} copy(bf16[256,8,729]{0,1,2:T(8,128)(2,1)} %param.8) | data formatting | bytes 5971968 | tf_op args[1]
  8.1 131.4 %shard_map.73 = bf16[2,8,32,729]{3,2,1,0:T(8,128)(2,1)} custom-call(f32[4,8]{1,0:T(4,128)} %pad_maximum_fusion.flags_ref, bf16[2,8,32,729]{3,2,1,0:T(8,128)(2,1)} %start_ref.1, bf16[8,256,729]{2,1,0:T(8,128)(2,1)} %bitcast.7, bf16[729,729]{1,0:T(8,128)(2,1)} %stiff_ref.1, f32[8,729]{1,0:T(8,128)} %pot_ref.1, s32[2,81]{1,0:T(2,128)} %and_select_fusion.face_ref), custom_call_target="tpu_custom_call" | custom-call | tf_op jit(solution)/shard_map/pallas_call | solution.py:434
  139.6 2.1 %copy.11 = bf16[2,8,32,729]{3,2,1,0:T(8,128)(2,1)} copy(bf16[2,8,32,729]{3,2,1,0:T(8,128)(2,1)} %shard_map.73) | data formatting | bytes 1492992
  (1 shorter events, 0.0 us)

commit v2 on v1

--- a/solution.py
+++ b/solution.py
@@ -29,9 +29,10 @@
 
 def kernel(
     sizes,
-    flags_ref,
+    scale_ref,
+    count_ref,
     start_ref,
-    res_ref,
+    res_hbm,
     stiff_ref,
     pot_ref,
     face_ref,
@@ -46,6 +47,12 @@
     proj,
     share,
     share_recv,
+    res_in,
+    res_wide,
+    res_ref,
+    res_near,
+    proj_near,
+    retained,
     face_out,
     face_in,
     face_send_sem,
@@ -58,8 +65,13 @@
     two_recv_sem,
     share_send_sem,
     share_recv_sem,
+    load_sem,
+    near_send_sem,
+    near_recv_sem,
+    coef_send_sem,
+    coef_recv_sem,
 ):
-    doms, sts, blocks, cells, width, nodes, face, res, rows = sizes
+    doms, sts, blocks, cells, width, nodes, face, res, rows, moved = sizes
     total_states = sts * width
     total_nodes = float(doms * cells * nodes)
     window = (nodes - face) // 128 * 128
@@ -70,6 +82,12 @@
     has_next, has_prev = d < doms - 1, d > 0
     own = pl.ds(pl.multiple_of(s * width, width), width)
     pending = []
+    count = count_ref[0]
+    scale = [scale_ref[c] for c in range(cells)]
+    live = [jnp.where(c < count, 1.0, 0.0).astype(F32) for c in range(cells)]
+    last = [jnp.where(c == count - 1, 1.0, 0.0).astype(F32) for c in range(cells)]
+    load = pltpu.make_async_copy(res_hbm, res_in, load_sem)
+    load.start()
 
     def dom_peer(k):
         return lax.rem(d + k, doms)
@@ -109,9 +127,34 @@
             device_id_type=pl.DeviceIdType.MESH,
         )
 
-    def one_hot(row, first, count):
-        node = lax.broadcasted_iota(jnp.int32, (count, face), 0) + first
-        return jnp.where(face_ref[row : row + 1, :] == node, 1.0, 0.0).astype(F32)
+    def one_hot(row, first, extent):
+        node = lax.broadcasted_iota(jnp.int32, (extent, face), 0) + first
+        if row == 0:
+            node = node + (count - 1) * nodes
+        return jnp.where(face_ref[0, row : row + 1, :] == node, 1.0, 0.0).astype(F32)
+
+    def mask(c):
+        return live[c].astype(BF16)
+
+    def relayout(chunk):
+        at = slice(chunk * face, (chunk + 1) * face)
+        wide = res_in[at].astype(F32).reshape(face * cells, res)
+        for h in range(res // 128):
+            lanes = slice(h * 128, (h + 1) * 128)
+            res_wide[h] = wide[:, lanes]
+            for c in range(cells):
+                res_ref[c, at, lanes] = res_wide[h, pl.ds(c, face, stride=cells), :].astype(BF16)
+
+    chunks = nodes // face
+
+    def first_chunks():
+        load.wait()
+        for chunk in range(chunks // 2):
+            relayout(chunk)
+
+    def last_chunks():
+        for chunk in range(chunks // 2, chunks):
+            relayout(chunk)
 
     def rows_of(c):
         return slice(c * width, (c + 1) * width)
@@ -126,15 +169,15 @@
             d + 1 if way == RIGHT else d - 1,
         )
 
-    def apply_operator(step, b, field):
+    def apply_operator(step, b, field, meanwhile=None):
         local[...] = dot_nn(field(None), stiff_ref[...])
         last_tail = jnp.zeros((width, nodes - window), F32)
         for c in range(cells):
-            value = flags_ref[0, c] * local[rows_of(c), :] + pot_ref[c : c + 1, :] * field(
+            value = scale[c] * local[rows_of(c), :] + pot_ref[c : c + 1, :] * field(
                 c
             ).astype(F32)
             local[rows_of(c), :] = value
-            last_tail = last_tail + flags_ref[3, c] * value[:, window:]
+            last_tail = last_tail + last[c] * value[:, window:]
         face_out[step, b, RIGHT] = dot_nn(
             last_tail, one_hot(0, window, nodes - window), lax.Precision.HIGHEST
         )
@@ -149,7 +192,7 @@
 
             pending.append((there, partial(face_copy, step, b, way)))
         for c in range(cells - 1):
-            pair = flags_ref[2, c + 1]
+            pair = live[c + 1]
             tail = local[rows_of(c), window:]
             head = local[rows_of(c + 1), :face]
             padded = head
@@ -157,6 +200,8 @@
                 padded = jnp.concatenate([jnp.zeros((width, offset), F32), head], axis=1)
             local[rows_of(c), window:] = tail + pair * padded
             local[rows_of(c + 1), :face] = head + pair * tail[:, offset:]
+        if meanwhile is not None:
+            meanwhile()
         for way, source in ((RIGHT, has_prev), (LEFT, has_next)):
 
             @pl.when(source)
@@ -174,27 +219,27 @@
             face_in[step, b, LEFT], one_hot(0, window, nodes - window), lax.Precision.HIGHEST
         )
         for c in range(cells):
-            local[rows_of(c), window:] += flags_ref[3, c] * tail_add
-
-    def filter_block(b):
+            local[rows_of(c), window:] += last[c] * tail_add
+
+    def filter_block(b, one=None, two=None):
         def first(c):
             if c is None:
                 parts = [first(i) for i in range(cells)]
                 return jnp.concatenate(parts, axis=0)
-            return start_ref[b, c] * flags_ref[1, c].astype(BF16)
+            return start_ref[b, c] * mask(c)
 
         def second(c):
             return inner[...] if c is None else inner[rows_of(c), :]
 
-        apply_operator(0, b, first)
+        apply_operator(0, b, first, one)
         for c in range(cells):
-            value = flags_ref[1, c] * local[rows_of(c), :]
+            value = live[c] * local[rows_of(c), :]
             inner[rows_of(c), :] = ((value - CENTER * first(c).astype(F32)) / HALF_WIDTH).astype(
                 BF16
             )
-        apply_operator(1, b, second)
+        apply_operator(1, b, second, two)
         for c in range(cells):
-            value = flags_ref[1, c] * local[rows_of(c), :]
+            value = live[c] * local[rows_of(c), :]
             states[b, c, own, :] = (
                 2.0 * (value - CENTER * second(c).astype(F32)) / HALF_WIDTH - first(c).astype(F32)
             ).astype(BF16)
@@ -239,7 +284,10 @@
 
         def add_cell(c, carry):
             block = states[b, c]
-            part[b, :res, :] += dot_nt(res_ref[c], block)
+            found = dot_nn(block, res_ref[c])
+            for h in range(res // total_states):
+                at = slice(h * total_states, (h + 1) * total_states)
+                part[b, at, :] += found[:, at]
             part[b, res : res + total_states, :] += dot_nt(block, block)
             return carry
 
@@ -309,87 +357,181 @@
         root_i, root_j = lax.rsqrt(along), lax.rsqrt(down)
         mixing = root_i * (1.5 * eye - 0.5 * (gram * root_i * root_j / total_nodes))
         mix[b] = mixing.astype(BF16)
-        proj[b] = dot_nt(mixing, total[b, :res, :], lax.Precision.HIGHEST).astype(BF16)
-
-    def share_copy(b, t, way):
-        return remote(
-            share.at[b, t],
-            share_recv.at[way, b, t],
-            share_send_sem.at[b, t],
-            share_recv_sem.at[way, b, t],
+        for h in range(res // total_states):
+            at = slice(h * total_states, (h + 1) * total_states)
+            proj[b, :, at] = dot_nn(mixing, total[b, at, :], lax.Precision.HIGHEST).astype(BF16)
+
+    def to(way):
+        return s + 1 if way == RIGHT else s - 1
+
+    origin = {RIGHT: s == 0, LEFT: s == sts - 1}
+    sends = {RIGHT: has_right, LEFT: has_left}
+    receives = {RIGHT: has_left, LEFT: has_right}
+    near_end = {RIGHT: s == 1, LEFT: s == sts - 2}
+    pieces = ((0, moved), (moved, cells))
+    both = jnp.logical_and
+
+    def near_copy(way, c):
+        return remote(
+            res_ref.at[c],
+            res_near.at[way, c],
+            near_send_sem.at[way, c],
+            near_recv_sem.at[way, c],
             "st",
-            s + 1 if way == RIGHT else s - 1,
+            to(way),
+        )
+
+    def near_start(c):
+        for way in (RIGHT, LEFT):
+            there = both(origin[way], sends[way])
+
+            @pl.when(there)
+            def _():
+                near_copy(way, c).start()
+
+            pending.append((there, partial(near_copy, way, c)))
+
+    def near_wait():
+        for way in (RIGHT, LEFT):
+
+            @pl.when(near_end[way])
+            def _():
+                for c in range(moved):
+                    near_copy(way, c).wait_recv()
+
+    def coef_copy(b, way):
+        return remote(
+            proj.at[b],
+            proj_near.at[way, b],
+            coef_send_sem.at[way, b],
+            coef_recv_sem.at[way, b],
+            "st",
+            to(way),
+        )
+
+    def coef_start(b):
+        for way in (RIGHT, LEFT):
+            there = both(origin[way], sends[way])
+
+            @pl.when(there)
+            def _():
+                coef_copy(b, way).start()
+
+            pending.append((there, partial(coef_copy, b, way)))
+
+    def share_copy(b, t, way, piece):
+        at = pl.ds(pieces[piece][0], pieces[piece][1] - pieces[piece][0])
+        return remote(
+            share.at[b, t, at],
+            share_recv.at[way, b, t, at],
+            share_send_sem.at[b, t, piece],
+            share_recv_sem.at[way, b, t, piece],
+            "st",
+            to(way),
         )
 
     def targets():
         for j in range(sts - 1):
             far = sts - 1 - j
-            yield far, RIGHT, far > s, has_left
-            yield j, LEFT, j < s, has_right
+            yield far, RIGHT, far > s
+            yield j, LEFT, j < s
 
     def share_start(b):
-        for t, way, ahead, behind in targets():
-
-            @pl.when(ahead)
-            def _():
-                def one(c, carry):
-                    share[b, t, c] = dot_nn(
-                        proj[b, t * width : (t + 1) * width, :], res_ref[c]
-                    ).astype(BF16)
-                    return carry
-
-                lax.fori_loop(0, cells, one, 0)
-
-            @pl.when(jnp.logical_and(ahead, jnp.logical_not(behind)))
-            def _():
-                share_copy(b, t, way).start()
-
-            pending.append((ahead, partial(share_copy, b, t, way)))
-
-    def share_forward(b):
-        for t, way, ahead, behind in targets():
-
-            @pl.when(jnp.logical_and(ahead, behind))
-            def _():
-                share_copy(b, t, way).wait_recv()
-
-                def one(c, carry):
-                    share[b, t, c] = (
-                        share[b, t, c].astype(F32) + share_recv[way, b, t, c].astype(F32)
-                    ).astype(BF16)
-                    return carry
-
-                lax.fori_loop(0, cells, one, 0)
-                share_copy(b, t, way).start()
-
-    def finish(b):
-        def own_copy(way):
-            return remote(
-                share.at[b, s],
-                share_recv.at[way, b, s],
-                share_send_sem.at[b, s],
-                share_recv_sem.at[way, b, s],
-                "st",
-                s + 1 if way == RIGHT else s - 1,
-            )
-
-        for c in range(cells):
-            local[rows_of(c), :] = dot_nn(mix[b, own, :], states[b, c]) - dot_nn(
+        def one(c, carry):
+            found = dot_nt(proj[b], res_ref[c])
+            for t in range(sts):
+                share[b, t, c] = found[t * width : (t + 1) * width, :].astype(BF16)
+            return carry
+
+        lax.fori_loop(0, cells, one, 0)
+        for t, way, ahead in targets():
+
+            @pl.when(both(ahead, origin[way]))
+            def _():
+                share_copy(b, t, way, 1).start()
+
+            for piece in (0, 1):
+                there = ahead if piece else both(ahead, jnp.logical_not(origin[way]))
+                pending.append((there, partial(share_copy, b, t, way, piece)))
+
+    def retain(b):
+        def one(c, carry):
+            retained[b, c] = dot_nn(mix[b, own, :], states[b, c]) - dot_nt(
                 proj[b, own, :], res_ref[c]
             )
-        for way, source in ((RIGHT, has_left), (LEFT, has_right)):
-
-            @pl.when(source)
-            def _():
-                own_copy(way).wait_recv()
-                for c in range(cells):
-                    local[rows_of(c), :] -= share_recv[way, b, s, c].astype(F32)
-
-        for c in range(cells):
-            out_ref[b, c] = local[rows_of(c), :].astype(BF16) * flags_ref[1, c].astype(BF16)
-
-    filter_block(0)
+            return carry
+
+        lax.fori_loop(0, cells, one, 0)
+
+    def near_share(b):
+        for way in (RIGHT, LEFT):
+
+            @pl.when(near_end[way])
+            def _():
+                coef_copy(b, way).wait_recv()
+                for c in range(moved):
+                    found = dot_nt(proj_near[way, b], res_near[way, c])
+                    for t in range(sts):
+                        passed = t > s if way == RIGHT else t < s
+
+                        @pl.when(passed)
+                        def _():
+                            share[b, t, c] = (
+                                share[b, t, c].astype(F32)
+                                + found[t * width : (t + 1) * width, :]
+                            ).astype(BF16)
+
+                        @pl.when(t == s)
+                        def _():
+                            retained[b, c] -= found[t * width : (t + 1) * width, :]
+
+    def share_forward(b):
+        for piece in (0, 1):
+            for t, way, ahead in targets():
+
+                @pl.when(both(ahead, jnp.logical_not(origin[way])))
+                def _():
+                    def absorb():
+                        share_copy(b, t, way, piece).wait_recv()
+
+                        def one(c, carry):
+                            share[b, t, c] = (
+                                share[b, t, c].astype(F32) + share_recv[way, b, t, c].astype(F32)
+                            ).astype(BF16)
+                            return carry
+
+                        lax.fori_loop(*pieces[piece], one, 0)
+
+                    if piece:
+                        absorb()
+                    else:
+                        pl.when(jnp.logical_not(near_end[way]))(absorb)
+                    share_copy(b, t, way, piece).start()
+
+    def finish(b):
+        for piece in (0, 1):
+            for way in (RIGHT, LEFT):
+                source = receives[way]
+                if piece == 0:
+                    source = both(source, jnp.logical_not(near_end[way]))
+
+                @pl.when(source)
+                def _():
+                    share_copy(b, s, way, piece).wait_recv()
+
+                    def one(c, carry):
+                        retained[b, c] -= share_recv[way, b, s, c].astype(F32)
+                        return carry
+
+                    lax.fori_loop(*pieces[piece], one, 0)
+
+            for c in range(*pieces[piece]):
+                out_ref[b, c] = retained[b, c].astype(BF16) * mask(c)
+
+    filter_block(0, first_chunks, last_chunks)
     gather_start(0)
+    for c in range(moved):
+        near_start(c)
     for b in range(1, blocks):
         filter_block(b)
     for b in range(blocks):
@@ -400,8 +542,13 @@
         all_reduce(b)
         if b:
             share_forward(b - 1)
+        else:
+            near_wait()
         coefficients(b)
+        coef_start(b)
         share_start(b)
+        retain(b)
+        near_share(b)
         if b:
             finish(b - 1)
     share_forward(blocks - 1)
@@ -423,18 +570,15 @@
     doms, sts = lax.axis_size("dom"), lax.axis_size("st")
     total_states = sts * width
     rows = -(-(res + total_states) // (8 * doms)) * 8
-    slot = jnp.arange(cells)
-    live = (slot < cell_count[0]).astype(F32)
-    last = (slot == cell_count[0] - 1).astype(F32)
-    flags = jnp.stack([cell_scale, live, live, last])
-    face_nodes = face_index[0] % nodes
-    sizes = (doms, sts, blocks, cells, width, nodes, face, res, rows)
+    moved = cells // 4
+    sizes = (doms, sts, blocks, cells, width, nodes, face, res, rows, moved)
     dma = pltpu.SemaphoreType.DMA
     vmem = pl.BlockSpec(memory_space=pltpu.VMEM)
+    smem = pl.BlockSpec(memory_space=pltpu.SMEM)
     return pl.pallas_call(
         partial(kernel, sizes),
         out_shape=jax.ShapeDtypeStruct((blocks, cells, width, nodes), BF16),
-        in_specs=[pl.BlockSpec(memory_space=pltpu.SMEM)] + [vmem] * 5,
+        in_specs=[smem, smem, vmem, pl.BlockSpec(memory_space=pl.ANY), vmem, vmem, vmem],
         out_specs=vmem,
         scratch_shapes=[
             pltpu.VMEM((cells * width, nodes), F32),
@@ -447,6 +591,12 @@
             pltpu.VMEM((blocks, total_states, res), BF16),
             pltpu.VMEM((blocks, sts, cells, width, nodes), BF16),
             pltpu.VMEM((2, blocks, sts, cells, width, nodes), BF16),
+            pltpu.VMEM((nodes, cells, res), BF16),
+            pltpu.VMEM((res // 128, face * cells, 128), F32),
+            pltpu.VMEM((cells, nodes, res), BF16),
+            pltpu.VMEM((2, moved, nodes, res), BF16),
+            pltpu.VMEM((2, blocks, total_states, res), BF16),
+            pltpu.VMEM((blocks, cells, width, nodes), F32),
             pltpu.VMEM((2, blocks, 2, width, face), F32),
             pltpu.VMEM((2, blocks, 2, width, face), F32),
             dma((2, blocks, 2)),
@@ -457,19 +607,25 @@
             dma((blocks, doms)),
             dma((blocks, doms)),
             dma((blocks, doms)),
-            dma((blocks, sts)),
-            dma((2, blocks, sts)),
+            dma((blocks, sts, 2)),
+            dma((2, blocks, sts, 2)),
+            dma,
+            dma((2, moved)),
+            dma((2, moved)),
+            dma((2, blocks)),
+            dma((2, blocks)),
         ],
         compiler_params=pltpu.CompilerParams(
             collective_id=0, has_side_effects=True, vmem_limit_bytes=60 * 1024 * 1024
         ),
     )(
-        flags,
+        cell_scale,
+        cell_count,
         start_block,
-        jnp.transpose(resident, (1, 0, 2)),
+        jnp.transpose(resident, (2, 1, 0)),
         stiffness,
         potential,
-        face_nodes,
+        face_index,
     )
 
 

time: 142 us -> 143 us (level)
  Pallas kernels: 131 us -> 140 us
  local copies, waits for them, and re-layouts: 7.06 us -> 2.06 us
  other arithmetic: 2.48 us -> 0 us
    pallas_call x1, Pallas kernels: 131 us -> 140 us  [on_device(): pl.pallas_call(partial(kernel, sizes), out_shape=jax.ShapeDtypeStruct((bl...]
    unnamed x2 -> x1, local copies, waits for them, and re-layouts: 7.06 us -> 2.06 us
where the time goes in v2:
time: 143 us
  Pallas kernels  140 us (98%)
  local copies, waits for them, and re-layouts  2.06 us (1%)
    pallas_call x1, Pallas kernels, on_device(): pl.pallas_call(partial(kernel, sizes), out_shape=jax.ShapeDtypeStruct((bl...  140 us

profile of v2, /device:TPU:0, one launch (start us, length us, event | category | flops | bytes accessed | tf_op | source)
XLA Modules:
  0.0 142.8 jit_solution(15089891214866128326)
XLA Ops:
  0.7 140.1 %shard_map.73 = bf16[2,8,32,729]{3,2,1,0:T(8,128)(2,1)} custom-call(f32[8]{0:T(128)} %scale_ref.1, s32[1]{0:T(128)S(6)} %copy.9.count_ref, bf16[2,8,32,729]{3,2,1,0:T(8,128)(2,1)} %start_ref.1, bf16[729,8,256]{2,1,0:T(8,128)(2,1)} %bitcast.1, bf16[729,729]{1,0:T(8,128)(2,1)} %stiff_ref.1, f32[8,729]{1,0:T(8,128)} %pot_ref.1, s32[1,2,81]{2,1,0:T(2,128)} %face_ref.1), custom_call_target="tpu_custom_call" | custom-call | tf_op jit(solution)/shard_map/pallas_call | solution.py:578
  140.7 2.1 %copy.10 = bf16[2,8,32,729]{3,2,1,0:T(8,128)(2,1)} copy(bf16[2,8,32,729]{3,2,1,0:T(8,128)(2,1)} %shard_map.73) | data formatting | bytes 1492992

commit v3 on v2

--- a/solution.py
+++ b/solution.py
@@ -82,6 +82,7 @@
     has_next, has_prev = d < doms - 1, d > 0
     own = pl.ds(pl.multiple_of(s * width, width), width)
     pending = []
+    both = jnp.logical_and
     count = count_ref[0]
     scale = [scale_ref[c] for c in range(cells)]
     live = [jnp.where(c < count, 1.0, 0.0).astype(F32) for c in range(cells)]
@@ -262,9 +263,9 @@
 
         pending.append((there, partial(gather_copy, b, way, shard)))
 
-    def gather_start(b):
-        gather_send(b, RIGHT, s, has_right)
-        gather_send(b, LEFT, s, has_left)
+    def gather_start(b, k):
+        gather_send(b, RIGHT, s, both(has_right, s == k))
+        gather_send(b, LEFT, s, both(has_left, s + k == sts - 1))
 
     def gather_steps(b):
         for k in range(1, sts):
@@ -277,7 +278,9 @@
                 def _():
                     gather_copy(b, way, shard).wait_recv()
 
-                gather_send(b, way, shard, jnp.logical_and(here, more))
+                gather_send(b, way, shard, both(here, more))
+            if b + 1 < blocks:
+                gather_start(b + 1, k)
 
     def contract(b):
         part[b] = jnp.zeros(part.shape[1:], F32)
@@ -369,7 +372,6 @@
     receives = {RIGHT: has_left, LEFT: has_right}
     near_end = {RIGHT: s == 1, LEFT: s == sts - 2}
     pieces = ((0, moved), (moved, cells))
-    both = jnp.logical_and
 
     def near_copy(way, c):
         return remote(
@@ -485,28 +487,27 @@
                         def _():
                             retained[b, c] -= found[t * width : (t + 1) * width, :]
 
-    def share_forward(b):
-        for piece in (0, 1):
-            for t, way, ahead in targets():
-
-                @pl.when(both(ahead, jnp.logical_not(origin[way])))
-                def _():
-                    def absorb():
-                        share_copy(b, t, way, piece).wait_recv()
-
-                        def one(c, carry):
-                            share[b, t, c] = (
-                                share[b, t, c].astype(F32) + share_recv[way, b, t, c].astype(F32)
-                            ).astype(BF16)
-                            return carry
-
-                        lax.fori_loop(*pieces[piece], one, 0)
-
-                    if piece:
-                        absorb()
-                    else:
-                        pl.when(jnp.logical_not(near_end[way]))(absorb)
-                    share_copy(b, t, way, piece).start()
+    def share_forward(b, piece):
+        for t, way, ahead in targets():
+
+            @pl.when(both(ahead, jnp.logical_not(origin[way])))
+            def _():
+                def absorb():
+                    share_copy(b, t, way, piece).wait_recv()
+
+                    def one(c, carry):
+                        share[b, t, c] = (
+                            share[b, t, c].astype(F32) + share_recv[way, b, t, c].astype(F32)
+                        ).astype(BF16)
+                        return carry
+
+                    lax.fori_loop(*pieces[piece], one, 0)
+
+                if piece:
+                    absorb()
+                else:
+                    pl.when(jnp.logical_not(near_end[way]))(absorb)
+                share_copy(b, t, way, piece).start()
 
     def finish(b):
         for piece in (0, 1):
@@ -529,29 +530,33 @@
                 out_ref[b, c] = retained[b, c].astype(BF16) * mask(c)
 
     filter_block(0, first_chunks, last_chunks)
-    gather_start(0)
+    for k in range(sts):
+        gather_start(0, k)
     for c in range(moved):
         near_start(c)
     for b in range(1, blocks):
         filter_block(b)
+    if blocks > 1:
+        gather_start(1, 0)
+    gather_steps(0)
     for b in range(blocks):
-        gather_steps(b)
-        if b + 1 < blocks:
-            gather_start(b + 1)
         contract(b)
         all_reduce(b)
         if b:
-            share_forward(b - 1)
-        else:
-            near_wait()
+            share_forward(b - 1, 1)
         coefficients(b)
         coef_start(b)
         share_start(b)
         retain(b)
+        if b + 1 < blocks:
+            gather_steps(b + 1)
+        if b == 0:
+            near_wait()
         near_share(b)
+        share_forward(b, 0)
         if b:
             finish(b - 1)
-    share_forward(blocks - 1)
+    share_forward(blocks - 1, 1)
     finish(blocks - 1)
     for there, make in pending:
 

time: 143 us -> 137 us (0.958)
  Pallas kernels: 140 us -> 134 us
    pallas_call x1, Pallas kernels: 140 us -> 134 us  [on_device(): pl.pallas_call(partial(kernel, sizes), out_shape=jax.ShapeDtypeStruct((bl...]
where the time goes in v3:
time: 137 us
  Pallas kernels  134 us (98%)
  local copies, waits for them, and re-layouts  2.06 us (2%)
    pallas_call x1, Pallas kernels, on_device(): pl.pallas_call(partial(kernel, sizes), out_shape=jax.ShapeDtypeStruct((bl...  134 us

profile of v3, /device:TPU:0, one launch (start us, length us, event | category | flops | bytes accessed | tf_op | source)
XLA Modules:
  0.0 137.1 jit_solution(17080093756711371348)
XLA Ops:
  0.7 134.3 %shard_map.73 = bf16[2,8,32,729]{3,2,1,0:T(8,128)(2,1)} custom-call(f32[8]{0:T(128)} %scale_ref.1, s32[1]{0:T(128)S(6)} %copy.9.count_ref, bf16[2,8,32,729]{3,2,1,0:T(8,128)(2,1)} %start_ref.1, bf16[729,8,256]{2,1,0:T(8,128)(2,1)} %bitcast.1, bf16[729,729]{1,0:T(8,128)(2,1)} %stiff_ref.1, f32[8,729]{1,0:T(8,128)} %pot_ref.1, s32[1,2,81]{2,1,0:T(2,128)} %face_ref.1), custom_call_target="tpu_custom_call" | custom-call | tf_op jit(solution)/shard_map/pallas_call | solution.py:583
  135.0 2.1 %copy.10 = bf16[2,8,32,729]{3,2,1,0:T(8,128)(2,1)} copy(bf16[2,8,32,729]{3,2,1,0:T(8,128)(2,1)} %shard_map.73) | data formatting | bytes 1492992

commit v4 on v3

--- a/solution.py
+++ b/solution.py
@@ -443,6 +443,11 @@
             found = dot_nt(proj[b], res_ref[c])
             for t in range(sts):
                 share[b, t, c] = found[t * width : (t + 1) * width, :].astype(BF16)
+
+                @pl.when(t == s)
+                def _():
+                    retained[b, c] = -found[t * width : (t + 1) * width, :]
+
             return carry
 
         lax.fori_loop(0, cells, one, 0)
@@ -458,9 +463,7 @@
 
     def retain(b):
         def one(c, carry):
-            retained[b, c] = dot_nn(mix[b, own, :], states[b, c]) - dot_nt(
-                proj[b, own, :], res_ref[c]
-            )
+            retained[b, c] += dot_nn(mix[b, own, :], states[b, c])
             return carry
 
         lax.fori_loop(0, cells, one, 0)
@@ -532,12 +535,13 @@
     filter_block(0, first_chunks, last_chunks)
     for k in range(sts):
         gather_start(0, k)
-    for c in range(moved):
-        near_start(c)
+    near_start(0)
     for b in range(1, blocks):
         filter_block(b)
     if blocks > 1:
         gather_start(1, 0)
+    for c in range(1, moved):
+        near_start(c)
     gather_steps(0)
     for b in range(blocks):
         contract(b)
@@ -547,13 +551,13 @@
         coefficients(b)
         coef_start(b)
         share_start(b)
-        retain(b)
         if b + 1 < blocks:
             gather_steps(b + 1)
         if b == 0:
             near_wait()
         near_share(b)
         share_forward(b, 0)
+        retain(b)
         if b:
             finish(b - 1)
     share_forward(blocks - 1, 1)
@@ -575,7 +579,7 @@
     doms, sts = lax.axis_size("dom"), lax.axis_size("st")
     total_states = sts * width
     rows = -(-(res + total_states) // (8 * doms)) * 8
-    moved = cells // 4
+    moved = 3 * cells // 8
     sizes = (doms, sts, blocks, cells, width, nodes, face, res, rows, moved)
     dma = pltpu.SemaphoreType.DMA
     vmem = pl.BlockSpec(memory_space=pltpu.VMEM)

time: 137 us -> 136 us (level)
  no operation moved by 1% of the time
where the time goes in v4:
time: 136 us
  Pallas kernels  133 us (98%)
  local copies, waits for them, and re-layouts  2.06 us (2%)
    pallas_call x1, Pallas kernels, on_device(): pl.pallas_call(partial(kernel, sizes), out_shape=jax.ShapeDtypeStruct((bl...  133 us

profile of v4, /device:TPU:0, one launch (start us, length us, event | category | flops | bytes accessed | tf_op | source)
XLA Modules:
  0.0 135.9 jit_solution(10770305501972007058)
XLA Ops:
  0.7 133.2 %shard_map.73 = bf16[2,8,32,729]{3,2,1,0:T(8,128)(2,1)} custom-call(f32[8]{0:T(128)} %scale_ref.1, s32[1]{0:T(128)S(6)} %copy.9.count_ref, bf16[2,8,32,729]{3,2,1,0:T(8,128)(2,1)} %start_ref.1, bf16[729,8,256]{2,1,0:T(8,128)(2,1)} %bitcast.1, bf16[729,729]{1,0:T(8,128)(2,1)} %stiff_ref.1, f32[8,729]{1,0:T(8,128)} %pot_ref.1, s32[1,2,81]{2,1,0:T(2,128)} %face_ref.1), custom_call_target="tpu_custom_call" | custom-call | tf_op jit(solution)/shard_map/pallas_call | solution.py:587
  133.8 2.1 %copy.10 = bf16[2,8,32,729]{3,2,1,0:T(8,128)(2,1)} copy(bf16[2,8,32,729]{3,2,1,0:T(8,128)(2,1)} %shard_map.73) | data formatting | bytes 1492992
